TPU v7x, 32 devices: a whole 2x2x4 slice. The times are simulated.
32 devices in a mesh: gx: 16 (over z, y, core), gz: 2 (over x).
Axes of the slice: x: 2, y: 2, z: 4, core: 2. Of those that a mesh axis runs over, the one named last changes fastest.
Arguments:
- density: float32 [4096, 8, 1024], P('gx', None, 'gz'), may hold values from 0.5 to 2
- momentum: float32 [3, 4096, 8, 1024], P(None, 'gx', None, 'gz'), may hold values from -3 to 3
- energy: float32 [4096, 8, 1024], P('gx', None, 'gz'), may hold values from 2 to 4
- costate: float32 [5, 4096, 8, 1024], P(None, 'gx', None, 'gz'), may hold values from -6 to 6
Outputs:
- adjoint: float32 [5, 4096, 8, 1024], P(None, 'gx', None, 'gz')
All inputs are finite; a program needn't handle non-finite values.
Results may differ from a plain program's by a relative error of at most 0.00005.
Values sent between devices are 32-bit elements; how exact they have to be, the bound alone decides.
A program may use at most 192 MiB of HBM per device.

v0:
```python
import functools
import math

import jax
import jax.numpy as jnp
import numpy as np
from jax import lax
from jax.experimental import pallas as pl
from jax.experimental.pallas import tpu as pltpu
from jax.sharding import PartitionSpec as P

pade_alpha = 1.0 / 3.0
step_scale = 0.1
root = (-1.0 + math.sqrt(1.0 - 4.0 * pade_alpha * pade_alpha)) / (2.0 * pade_alpha)
near = step_scale / 12.0
tail = -step_scale * 25.0 / 12.0


def split(values):
    high = values.astype(jnp.bfloat16)
    low = (values - high.astype(jnp.float32)).astype(jnp.bfloat16)
    return high, low


def toeplitz(size):
    gap = np.arange(size)[:, None] - np.arange(size)[None, :]
    weight = tail * np.power(-root, np.abs(gap)) * np.where(gap % 2 == 0, 1.0, -1.0)
    weight = weight + near * (np.abs(gap) == 1)
    return np.sign(gap) * weight


def span_weights(length):
    block = min(256, length)
    inside = toeplitz(block)
    half = np.arange(block) < block // 2
    corner = inside * (half[:, None] != half[None, :])
    both = jnp.asarray(np.stack([inside, corner]).astype(np.float32))
    return jnp.stack(split(both))


def summary_weights():
    lane = np.arange(128)
    signed = lambda power: np.power(-root, power) * np.where(power % 2 == 0, 1.0, -1.0)
    rows = np.zeros((2, 8, 128), np.float32)
    rows[0, 0] = signed(lane + 1)
    rows[0, 1, 0] = 1.0
    rows[1, 0] = signed(128 - lane)
    rows[1, 1, 127] = 1.0
    return jnp.concatenate(split(jnp.asarray(rows)), 1)


def rim_weights():
    lane = np.arange(128)
    signed = lambda power: np.power(-root, power) * np.where(power % 2 == 0, 1.0, -1.0)
    rows = np.zeros((4, 256), np.float32)
    rows[0, :128] = -tail * signed(lane)
    rows[1, 0] = -near
    rows[2, 128:] = tail * signed(127 - lane)
    rows[3, 255] = near
    high, low = split(jnp.asarray(rows))
    return jnp.concatenate([high, high, low, jnp.zeros_like(high)])


def edges_kernel(
    chunks, rows, cost_ref, weight_ref, ahead_ref, up_ref, down_ref, zup_ref, zdown_ref,
):
    step = pl.program_id(0)
    fields = cost_ref.shape[0]
    lanes = cost_ref.shape[3]

    @pl.when(step == 0)
    def _():
        up_ref[...] = jnp.zeros_like(up_ref)
        down_ref[...] = jnp.zeros_like(down_ref)
        up_ref[1] = cost_ref[:, rows - 1]

    ahead_ref[0] = down_ref[...]
    scale = jnp.float32(0.0)
    heard = [k for k in range(chunks) if abs(root ** (rows * k)) > 1e-38]
    for k in heard:
        scale = jnp.where(step == k, jnp.float32(root ** (rows * k)), scale)

    @pl.when(step < len(heard))
    def _():
        fronts = [jnp.zeros_like(up_ref[0, f]) for f in range(fields)]
        for i in range(rows):
            fronts = [root * (cost_ref[f, i] + fronts[f]) for f in range(fields)]
        for f in range(fields):
            up_ref[0, f] = up_ref[0, f] + scale * fronts[f]

    contract = functools.partial(
        lax.dot_general, dimension_numbers=(((1,), (1,)), ((), ())),
        preferred_element_type=jnp.float32,
    )
    backs = [down_ref[0, f] for f in range(fields)]
    for i in reversed(range(rows)):
        backs = [root * (cost_ref[f, i] + backs[f]) for f in range(fields)]
    for field in range(fields):
        down_ref[0, field] = backs[field]
        down_ref[1, field] = cost_ref[field, 0]
        at = pl.ds(field * rows * 8, rows * 8)
        for side, from_lane, ref in ((0, 0, zdown_ref), (1, lanes - 128, zup_ref)):
            part = cost_ref[field, :, :, from_lane : from_lane + 128]
            high, low = split(part.reshape(rows * 8, 128))
            both = contract(weight_ref[side], high)
            ref[0, :, at] = both[0:2] + both[8:10] + contract(weight_ref[side], low)[0:2]


def edges(costate, rows):
    fields, length, planes, lanes = costate.shape
    chunks = length // rows
    flat = fields * rows * planes
    layer = (2, fields, planes, lanes)
    reverse = lambda s: chunks - 1 - s
    f32 = jnp.float32
    return pl.pallas_call(
        functools.partial(edges_kernel, chunks, rows),
        grid=(chunks,),
        in_specs=[
            pl.BlockSpec((fields, rows, planes, lanes), lambda s: (0, reverse(s), 0, 0)),
            pl.BlockSpec((2, 16, 128), lambda s: (0, 0, 0)),
        ],
        out_specs=[
            pl.BlockSpec((1,) + layer, lambda s: (reverse(s), 0, 0, 0, 0)),
            pl.BlockSpec(layer, lambda s: (0, 0, 0, 0)),
            pl.BlockSpec(layer, lambda s: (0, 0, 0, 0)),
            pl.BlockSpec((1, 2, flat), lambda s: (reverse(s), 0, 0)),
            pl.BlockSpec((1, 2, flat), lambda s: (reverse(s), 0, 0)),
        ],
        out_shape=[
            jax.ShapeDtypeStruct((chunks,) + layer, f32),
            jax.ShapeDtypeStruct(layer, f32),
            jax.ShapeDtypeStruct(layer, f32),
            jax.ShapeDtypeStruct((chunks, 2, flat), f32),
            jax.ShapeDtypeStruct((chunks, 2, flat), f32),
        ],
        name="edges",
    )(costate, summary_weights())


def pulled_back(density, momentum, energy, a, b):
    inverse = 1.0 / density
    u, v, w = (m * inverse for m in momentum)
    square = u * u + v * v + w * w
    fifth = 0.2 * square
    h = 1.4 * (energy * inverse) - fifth
    along = a[1] * u + a[2] * v + a[3] * w + a[4] * h
    across = b[1] * u + b[2] * v + b[3] * w + b[4] * h
    work = a[4] * u + b[4] * w
    push = work + a[1] + b[3]
    q = 0.4 * push
    return (
        fifth * push - (u * along + w * across),
        a[0] + along + (a[1] - q) * u + b[1] * w,
        a[2] * u + b[2] * w - q * v,
        b[0] + across + a[3] * u + (b[3] - q) * w,
        work + q,
    )


def main_kernel(
    chunks, rows, density_ref, momentum_ref, energy_ref, cost_ref, ahead_ref,
    left_ref, right_ref, zleft_ref, zright_ref, weight_ref, rim_ref,
    out_ref, back_ref, span_ref, carry_ref,
):
    step = pl.program_id(0)
    fields, _, planes, lanes = cost_ref.shape
    block = weight_ref.shape[2]
    f32 = jnp.float32

    @pl.when(step == 0)
    def _():
        carry_ref[...] = left_ref[...]

    last = step == chunks - 1
    scale = f32(0.0)
    for k in range(chunks):
        scale = jnp.where(step == k, f32(root ** (rows * (chunks - 1 - k))), scale)
    keep = jnp.where(last, f32(1.0), f32(0.0))

    def times(high, low, kind):
        dot = functools.partial(jnp.dot, preferred_element_type=f32)
        heavy, light = weight_ref[0, kind], weight_ref[1, kind]
        return dot(high, heavy) + dot(low, heavy) + dot(high, light)

    flat = rows * planes
    turned = (((0,), (0,)), ((), ()))
    rim = jnp.concatenate([zleft_ref[0], zright_ref[0]], 0)
    rim_high = rim.astype(jnp.bfloat16).astype(f32)
    rim = jnp.concatenate([rim_high, rim - rim_high, rim_high, jnp.zeros_like(rim)], 0)
    rim = rim.astype(jnp.bfloat16)
    for field in range(fields):
        high, low = split(cost_ref[field].reshape(flat, lanes))
        tiles = []
        for at in range(0, lanes, block):
            part = times(high[:, at : at + block], low[:, at : at + block], 0)
            tiles += [part[:, t : t + 128] for t in range(0, block, 128)]
        for at in range(block // 2, lanes - block // 2, block):
            if at + block > lanes:
                break
            part = times(high[:, at : at + block], low[:, at : at + block], 1)
            for t in range(0, block, 128):
                tiles[(at + t) // 128] += part[:, t : t + 128]
        at = field * flat
        part = lax.dot_general(
            rim[:, at : at + flat], rim_ref[...], turned, preferred_element_type=f32
        )
        tiles[0] += part[:, :128]
        tiles[-1] += part[:, 128:]
        for t, tile in enumerate(tiles):
            span_ref[field, :, :, t * 128 : (t + 1) * 128] = tile.reshape(rows, planes, 128)
        back = ahead_ref[0, 0, field] + scale * right_ref[0, field]
        ahead = ahead_ref[0, 1, field] + keep * right_ref[1, field]
        for i in reversed(range(rows)):
            back_ref[field, i] = tail * back + near * ahead
            ahead = cost_ref[field, i]
            back = root * (ahead + back)

    for t in range(lanes // 128):
        at = slice(t * 128, (t + 1) * 128)

        def body(i, carried):
            fronts, befores = carried
            here = [cost_ref[f, i, :, at] for f in range(fields)]
            a = [
                back_ref[f, i, :, at] - (tail * fronts[f] + near * befores[f])
                for f in range(fields)
            ]
            b = [span_ref[f, i, :, at] for f in range(fields)]
            pulled = pulled_back(
                density_ref[i, :, at],
                [momentum_ref[k, i, :, at] for k in range(3)],
                energy_ref[i, :, at],
                a, b,
            )
            for f in range(fields):
                out_ref[f, i, :, at] = here[f] + pulled[f]
            return ([root * (p + q) for p, q in zip(here, fronts)], here)

        start = (
            [carry_ref[0, f, :, at] for f in range(fields)],
            [carry_ref[1, f, :, at] for f in range(fields)],
        )
        fronts, befores = lax.fori_loop(0, rows, body, start, unroll=8)
        for f in range(fields):
            carry_ref[0, f, :, at] = fronts[f]
            carry_ref[1, f, :, at] = befores[f]


def main(density, momentum, energy, costate, ahead, left, right, zleft, zright, rows):
    fields, length, planes, lanes = costate.shape
    chunks = length // rows
    flat = fields * rows * planes
    layer = (2, fields, planes, lanes)
    weights, rim = span_weights(lanes), rim_weights()
    whole = lambda array: pl.BlockSpec(array.shape, lambda s: (0,) * array.ndim)
    state = pl.BlockSpec((rows, planes, lanes), lambda s: (s, 0, 0))
    stacked = lambda k: pl.BlockSpec((k, rows, planes, lanes), lambda s: (0, s, 0, 0))
    strip = pl.BlockSpec((1, 2, flat), lambda s: (s, 0, 0))
    f32 = jnp.float32
    return pl.pallas_call(
        functools.partial(main_kernel, chunks, rows),
        grid=(chunks,),
        in_specs=[
            state, stacked(3), state, stacked(fields),
            pl.BlockSpec((1,) + layer, lambda s: (s, 0, 0, 0, 0)),
            whole(left), whole(right), strip, strip, whole(weights), whole(rim),
        ],
        out_specs=stacked(fields),
        out_shape=jax.ShapeDtypeStruct(costate.shape, f32),
        scratch_shapes=[
            pltpu.VMEM((fields, rows, planes, lanes), f32),
            pltpu.VMEM((fields, rows, planes, lanes), f32),
            pltpu.VMEM(layer, f32),
        ],
        name="pull",
    )(density, momentum, energy, costate, ahead, left, right, zleft, zright, weights, rim)


def per_device(density, momentum, energy, costate):
    rows = 32
    ahead, up, down, zup, zdown = edges(costate, rows)

    def shifted(values, axis, by):
        peers = lax.axis_size(axis)
        return lax.ppermute(values, axis, [(i, (i + by) % peers) for i in range(peers)])

    left = shifted(up, "gx", 1)
    right = shifted(down, "gx", -1)
    zleft = shifted(zup, "gz", 1)
    zright = shifted(zdown, "gz", -1)
    return main(density, momentum, energy, costate, ahead, left, right, zleft, zright, rows)


def solution(mesh):
    return jax.shard_map(
        per_device,
        mesh=mesh,
        in_specs=(
            P("gx", None, "gz"),
            P(None, "gx", None, "gz"),
            P("gx", None, "gz"),
            P(None, "gx", None, "gz"),
        ),
        out_specs=P(None, "gx", None, "gz"),
        check_vma=False,
    )
```

profile of v0, /device:TPU:0, one launch (start us, length us, event | category | flops | bytes accessed | tf_op | source)
XLA Modules:
  0.0 58.7 jit_solution(13501771343132314140)
XLA Ops:
  0.0 11.5 %edges.1 = (f32[8,2,5,8,512]{4,3,2,1,0:T(8,128)}, f32[2,5,8,512]{3,2,1,0:T(8,128)}, f32[2,5,8,512]{3,2,1,0:T(8,128)}, f32[8,2,1280]{2,1,0:T(2,128)}, f32[8,2,1280]{2,1,0:T(2,128)}) custom-call(f32[5,256,8,512]{3,2,1,0:T(8,128)} %cost_ref.3, bf16[2,16,128]{2,1,0:T(8,128)(2,1)} %constant.15.weight_ref), custom_call_target="tpu_custom_call" | custom-call | tf_op jit(solution)/shard_map/edges/pallas_call | solution.py:116
  11.5 0.5 collective-permute-start
  12.1 5.0 %collective-permute-start.1 = (f32[2,5,8,512]{3,2,1,0:T(8,128)}, f32[2,5,8,512]{3,2,1,0:T(8,128)S(1)}, u32[]{:S(2)}, u32[]{:S(2)}) collective-permute-start(f32[2,5,8,512]{3,2,1,0:T(8,128)} %get-tuple-element.12), channel_id=1, source_target_pairs={{0,30},{2,0},{4,2},{6,4},{8,6},{10,8},{12,10},{14,12},{16,14},{18,... | collective-permute-start | bytes 491528 | tf_op jit(solution)/shard_map/ppermute | solution.py:286
  17.1 1.9 %collective-permute-start.2 = (f32[8,2,1280]{2,1,0:T(2,128)}, f32[8,2,1280]{2,1,0:T(2,128)S(1)}, u32[]{:S(2)}, u32[]{:S(2)}) collective-permute-start(f32[8,2,1280]{2,1,0:T(2,128)} %get-tuple-element.13), channel_id=1, source_target_pairs={{0,1},{1,0},{2,3},{3,2},{4,5},{5,4},{6,7},{7,6},{8,9},{9,8},{10,11... | collective-permute-start | bytes 245768 | tf_op jit(solution)/shard_map/ppermute | solution.py:286
  19.0 0.2 collective-permute-start.3
  19.2 2.6 %collective-permute-done.2.zleft_ref = f32[8,2,1280]{2,1,0:T(2,128)S(1)} collective-permute-done((f32[8,2,1280]{2,1,0:T(2,128)}, f32[8,2,1280]{2,1,0:T(2,128)S(1)}, u32[]{:S(2)}, u32[]{:S(2)}) %collective-permute-start.2) | collective-permute-done | bytes 81952 | tf_op jit(solution)/shard_map/ppermute | solution.py:286
  21.8 0.0 copy-start.2
  21.8 1.9 %collective-permute-done.3.zright_ref = f32[8,2,1280]{2,1,0:T(2,128)S(1)} collective-permute-done((f32[8,2,1280]{2,1,0:T(2,128)}, f32[8,2,1280]{2,1,0:T(2,128)S(1)}, u32[]{:S(2)}, u32[]{:S(2)}) %collective-permute-start.3) | collective-permute-done | bytes 81952 | tf_op jit(solution)/shard_map/ppermute | solution.py:286
  23.7 0.0 copy-start.3
  23.7 0.0 collective-permute-done.left_ref
  23.7 0.0 copy-start
  23.7 0.0 collective-permute-done.1.right_ref
  23.7 0.0 copy-start.1
  23.7 0.0 copy-done.2
  23.7 0.6 %copy-done.3 = f32[8,2,1280]{2,1,0:T(2,128)} copy-done((f32[8,2,1280]{2,1,0:T(2,128)}, f32[8,2,1280]{2,1,0:T(2,128)S(1)}, u32[]{:S(2)}) %copy-start.3) | copy-done | bytes 81944
  24.3 0.1 copy-done
  24.4 0.1 copy-done.1
  24.4 34.2 %pull.1 = f32[5,256,8,512]{3,2,1,0:T(8,128)} custom-call(f32[256,8,512]{2,1,0:T(8,128)} %density_ref.1, f32[3,256,8,512]{3,2,1,0:T(8,128)} %momentum_ref.1, f32[256,8,512]{2,1,0:T(8,128)} %energy_ref.1, f32[5,256,8,512]{3,2,1,0:T(8,128)} %cost_ref.3, f32[8,2,5,8,512]{4,3,2,1,0:T(8,128)} %get-tuple-element.10.ahead_ref, f32[2,5,8,512]{3,2,1,0:T(8,128)} %copy-done, ...), custom_call_target="tpu_custom_call" | custom-call | tf_op jit(solution)/shard_map/pull/pallas_call | solution.py:261
Async XLA Ops:
  11.5 12.1 %collective-permute-start = (f32[2,5,8,512]{3,2,1,0:T(8,128)}, f32[2,5,8,512]{3,2,1,0:T(8,128)S(1)}, u32[]{:S(2)}, u32[]{:S(2)}) collective-permute-start(f32[2,5,8,512]{3,2,1,0:T(8,128)} %get-tuple-element.11), channel_id=1, source_target_pairs={{0,2},{2,4},{4,6},{6,8},{8,10},{10,12},{12,14},{14,16},{16,18},{18... | collective-permute-start | bytes 491528 | tf_op jit(solution)/shard_map/ppermute | solution.py:286
  12.1 11.6 %collective-permute-start.1 = (f32[2,5,8,512]{3,2,1,0:T(8,128)}, f32[2,5,8,512]{3,2,1,0:T(8,128)S(1)}, u32[]{:S(2)}, u32[]{:S(2)}) collective-permute-start(f32[2,5,8,512]{3,2,1,0:T(8,128)} %get-tuple-element.12), channel_id=1, source_target_pairs={{0,30},{2,0},{4,2},{6,4},{8,6},{10,8},{12,10},{14,12},{16,14},{18,... | collective-permute-start | bytes 491528 | tf_op jit(solution)/shard_map/ppermute | solution.py:286
  17.1 4.7 %collective-permute-start.2 = (f32[8,2,1280]{2,1,0:T(2,128)}, f32[8,2,1280]{2,1,0:T(2,128)S(1)}, u32[]{:S(2)}, u32[]{:S(2)}) collective-permute-start(f32[8,2,1280]{2,1,0:T(2,128)} %get-tuple-element.13), channel_id=1, source_target_pairs={{0,1},{1,0},{2,3},{3,2},{4,5},{5,4},{6,7},{7,6},{8,9},{9,8},{10,11... | collective-permute-start | bytes 245768 | tf_op jit(solution)/shard_map/ppermute | solution.py:286
  19.0 4.7 %collective-permute-start.3 = (f32[8,2,1280]{2,1,0:T(2,128)}, f32[8,2,1280]{2,1,0:T(2,128)S(1)}, u32[]{:S(2)}, u32[]{:S(2)}) collective-permute-start(f32[8,2,1280]{2,1,0:T(2,128)} %get-tuple-element.14), channel_id=1, source_target_pairs={{0,1},{1,0},{2,3},{3,2},{4,5},{5,4},{6,7},{7,6},{8,9},{9,8},{10,11... | collective-permute-start | bytes 245768 | tf_op jit(solution)/shard_map/ppermute | solution.py:286
  21.8 1.9 %copy-start.2 = (f32[8,2,1280]{2,1,0:T(2,128)}, f32[8,2,1280]{2,1,0:T(2,128)S(1)}, u32[]{:S(2)}) copy-start(f32[8,2,1280]{2,1,0:T(2,128)S(1)} %collective-permute-done.2.zleft_ref) | copy-start | bytes 245764
  23.7 0.6 %copy-start.3 = (f32[8,2,1280]{2,1,0:T(2,128)}, f32[8,2,1280]{2,1,0:T(2,128)S(1)}, u32[]{:S(2)}) copy-start(f32[8,2,1280]{2,1,0:T(2,128)S(1)} %collective-permute-done.3.zright_ref) | copy-start | bytes 245764
  23.7 0.7 %copy-start = (f32[2,5,8,512]{3,2,1,0:T(8,128)}, f32[2,5,8,512]{3,2,1,0:T(8,128)S(1)}, u32[]{:S(2)}) copy-start(f32[2,5,8,512]{3,2,1,0:T(8,128)S(1)} %collective-permute-done.left_ref) | copy-start | bytes 491524
  23.7 0.7 %copy-start.1 = (f32[2,5,8,512]{3,2,1,0:T(8,128)}, f32[2,5,8,512]{3,2,1,0:T(8,128)S(1)}, u32[]{:S(2)}) copy-start(f32[2,5,8,512]{3,2,1,0:T(8,128)S(1)} %collective-permute-done.1.right_ref) | copy-start | bytes 491524
where the time goes:
time: 58.9 us; the launch traced here: 58.7 us
  Pallas kernels  45.8 us (78%)
  starting transfers between devices  7.62 us (13%)
  waiting for transfers between devices  4.5 us (8%)
  local copies, waits for them, and re-layouts  0.73 us (1%)
    pallas_call x1, Pallas kernels, main(): pl.pallas_call(functools.partial(main_kernel, chunks, rows), grid=(chunks...  34.2 us
    pallas_call x1, Pallas kernels, edges(): pl.pallas_call(functools.partial(edges_kernel, chunks, rows), grid=(chunk...  11.5 us
    ppermute x4, starting transfers between devices, shifted(): lax.ppermute(values, axis, [(i, (i + by) % peers) for i in range(peers)])  7.62 us
    ppermute x4, waiting for transfers between devices, shifted(): lax.ppermute(values, axis, [(i, (i + by) % peers) for i in range(peers)])  4.5 us
  transfers between devices with their start and end apart: 4, of which 2 were waited for; matrix products, arithmetic and copies ran while one was open for 0% of the time, Pallas kernels for 0%

commit v1 on v0

--- a/solution.py
+++ b/solution.py
@@ -61,81 +61,183 @@
     return jnp.concatenate([high, high, low, jnp.zeros_like(high)])
 
 
+def heard(chunks, rows):
+    return [k for k in range(chunks) if abs(root ** (rows * k)) > 1e-38]
+
+
+def decay(rows, k, at):
+    scale = jnp.float32(0.0)
+    for n in k:
+        scale = jnp.where(at == n, jnp.float32(root ** (rows * n)), scale)
+    return scale
+
+
+def visit(step, chunks):
+    return jnp.where(step % 2 == 0, chunks - 1 - step // 2, step // 2)
+
+
 def edges_kernel(
-    chunks, rows, cost_ref, weight_ref, ahead_ref, up_ref, down_ref, zup_ref, zdown_ref,
+    chunks, rows, cost_ref, weight_ref, raw_ref,
+    ahead_ref, left_ref, right_ref, zleft_ref, zright_ref,
+    up_ref, down_ref, local_ref, far_ref, zup_ref, zdown_ref, send, recv,
 ):
     step = pl.program_id(0)
     fields = cost_ref.shape[0]
     lanes = cost_ref.shape[3]
+    length = raw_ref.shape[1]
+    near_rows = heard(chunks, rows)
+    ready = min(2 * len(near_rows), chunks)
+
+    def shifted(axis, by):
+        peers = lax.axis_size(axis)
+        return {axis: lax.rem(lax.axis_index(axis) + (by + peers), peers)}
+
+    after, before = shifted("gx", 1), shifted("gx", -1)
+    zafter, zbefore = shifted("gz", 1), shifted("gz", -1)
+
+    def remote(source, target, k, device):
+        return pltpu.make_async_remote_copy(
+            src_ref=source, dst_ref=target, send_sem=send.at[k], recv_sem=recv.at[k],
+            device_id=device, device_id_type=pl.DeviceIdType.MESH,
+        )
+
+    rim_copies = [
+        remote(raw_ref.at[:, length - 1], left_ref.at[1], 0, after),
+        remote(raw_ref.at[:, 0], right_ref, 1, before),
+    ]
+    state_copies = [
+        remote(up_ref, left_ref.at[0], 2, after),
+        remote(down_ref, far_ref, 3, before),
+    ]
+
+    def span_copies(at):
+        chunk = visit(at, chunks)
+        return [
+            remote(zup_ref.at[chunk], zleft_ref.at[chunk], 4 + at, zafter),
+            remote(zdown_ref.at[chunk], zright_ref.at[chunk], 4 + chunks + at, zbefore),
+        ]
 
     @pl.when(step == 0)
     def _():
+        barrier = pltpu.get_barrier_semaphore()
+        for device in (after, before, zafter, zbefore):
+            pl.semaphore_signal(
+                barrier, inc=1, device_id=device, device_id_type=pl.DeviceIdType.MESH
+            )
         up_ref[...] = jnp.zeros_like(up_ref)
         down_ref[...] = jnp.zeros_like(down_ref)
-        up_ref[1] = cost_ref[:, rows - 1]
-
-    ahead_ref[0] = down_ref[...]
-    scale = jnp.float32(0.0)
-    heard = [k for k in range(chunks) if abs(root ** (rows * k)) > 1e-38]
-    for k in heard:
-        scale = jnp.where(step == k, jnp.float32(root ** (rows * k)), scale)
-
-    @pl.when(step < len(heard))
-    def _():
-        fronts = [jnp.zeros_like(up_ref[0, f]) for f in range(fields)]
-        for i in range(rows):
-            fronts = [root * (cost_ref[f, i] + fronts[f]) for f in range(fields)]
+
+    @pl.when(step == 1)
+    def _():
+        pl.semaphore_wait(pltpu.get_barrier_semaphore(), 4)
+        for copy in rim_copies:
+            copy.start()
+
+    @pl.when(step >= 1)
+    def _():
+        for copy in span_copies(step - 1):
+            copy.start()
+
+    @pl.when(step == ready)
+    def _():
+        for copy in state_copies:
+            copy.start()
+
+    @pl.when(step < chunks)
+    def _():
+        chunk = visit(step, chunks)
+        from_end = chunks - 1 - chunk
+
+        @pl.when(from_end < len(near_rows))
+        def _():
+            scale = decay(rows, near_rows, from_end)
+            fronts = [jnp.zeros_like(up_ref[f]) for f in range(fields)]
+            for i in range(rows):
+                fronts = [root * (cost_ref[f, i] + fronts[f]) for f in range(fields)]
+            for f in range(fields):
+                up_ref[f] = up_ref[f] + scale * fronts[f]
+
+        contract = functools.partial(
+            lax.dot_general, dimension_numbers=(((1,), (1,)), ((), ())),
+            preferred_element_type=jnp.float32,
+        )
+        backs = [jnp.zeros_like(down_ref[f]) for f in range(fields)]
+        for i in reversed(range(rows)):
+            backs = [root * (cost_ref[f, i] + backs[f]) for f in range(fields)]
+        scale = decay(rows, near_rows, chunk)
+        for field in range(fields):
+            local_ref[chunk, field] = backs[field]
+
+            @pl.when(chunk < len(near_rows))
+            def _():
+                down_ref[field] = down_ref[field] + scale * backs[field]
+
+            at = pl.ds(field * rows * 8, rows * 8)
+            for side, from_lane, ref in ((0, 0, zdown_ref), (1, lanes - 128, zup_ref)):
+                part = cost_ref[field, :, :, from_lane : from_lane + 128]
+                high, low = split(part.reshape(rows * 8, 128))
+                both = contract(weight_ref[side], high)
+                ref[chunk, :, at] = (
+                    both[0:2] + both[8:10] + contract(weight_ref[side], low)[0:2]
+                )
+
+    @pl.when(step == chunks)
+    def _():
+        for copy in rim_copies + state_copies:
+            copy.wait()
         for f in range(fields):
-            up_ref[0, f] = up_ref[0, f] + scale * fronts[f]
-
-    contract = functools.partial(
-        lax.dot_general, dimension_numbers=(((1,), (1,)), ((), ())),
-        preferred_element_type=jnp.float32,
-    )
-    backs = [down_ref[0, f] for f in range(fields)]
-    for i in reversed(range(rows)):
-        backs = [root * (cost_ref[f, i] + backs[f]) for f in range(fields)]
-    for field in range(fields):
-        down_ref[0, field] = backs[field]
-        down_ref[1, field] = cost_ref[field, 0]
-        at = pl.ds(field * rows * 8, rows * 8)
-        for side, from_lane, ref in ((0, 0, zdown_ref), (1, lanes - 128, zup_ref)):
-            part = cost_ref[field, :, :, from_lane : from_lane + 128]
-            high, low = split(part.reshape(rows * 8, 128))
-            both = contract(weight_ref[side], high)
-            ref[0, :, at] = both[0:2] + both[8:10] + contract(weight_ref[side], low)[0:2]
+            state = far_ref[f]
+            ahead_ref[chunks - 1, f] = state
+            for k in reversed(range(chunks - 1)):
+                state = local_ref[k + 1, f] + (root**rows) * state
+                ahead_ref[k, f] = state
+        for at in range(chunks):
+            for copy in span_copies(at):
+                copy.wait()
 
 
 def edges(costate, rows):
     fields, length, planes, lanes = costate.shape
     chunks = length // rows
     flat = fields * rows * planes
-    layer = (2, fields, planes, lanes)
-    reverse = lambda s: chunks - 1 - s
+    layer = (fields, planes, lanes)
     f32 = jnp.float32
+    anywhere = pl.BlockSpec(memory_space=pl.ANY)
     return pl.pallas_call(
         functools.partial(edges_kernel, chunks, rows),
-        grid=(chunks,),
+        grid=(chunks + 1,),
         in_specs=[
-            pl.BlockSpec((fields, rows, planes, lanes), lambda s: (0, reverse(s), 0, 0)),
+            pl.BlockSpec(
+                (fields, rows, planes, lanes),
+                lambda s: (0, visit(jnp.minimum(s, chunks - 1), chunks), 0, 0),
+            ),
             pl.BlockSpec((2, 16, 128), lambda s: (0, 0, 0)),
+            anywhere,
         ],
         out_specs=[
-            pl.BlockSpec((1,) + layer, lambda s: (reverse(s), 0, 0, 0, 0)),
-            pl.BlockSpec(layer, lambda s: (0, 0, 0, 0)),
-            pl.BlockSpec(layer, lambda s: (0, 0, 0, 0)),
-            pl.BlockSpec((1, 2, flat), lambda s: (reverse(s), 0, 0)),
-            pl.BlockSpec((1, 2, flat), lambda s: (reverse(s), 0, 0)),
+            pl.BlockSpec((chunks,) + layer, lambda s: (0, 0, 0, 0)),
+            anywhere, anywhere, anywhere, anywhere,
         ],
         out_shape=[
             jax.ShapeDtypeStruct((chunks,) + layer, f32),
-            jax.ShapeDtypeStruct(layer, f32),
+            jax.ShapeDtypeStruct((2,) + layer, f32),
             jax.ShapeDtypeStruct(layer, f32),
             jax.ShapeDtypeStruct((chunks, 2, flat), f32),
             jax.ShapeDtypeStruct((chunks, 2, flat), f32),
         ],
+        scratch_shapes=[
+            pltpu.VMEM(layer, f32),
+            pltpu.VMEM(layer, f32),
+            pltpu.VMEM((chunks,) + layer, f32),
+            pltpu.VMEM(layer, f32),
+            pltpu.VMEM((chunks, 2, flat), f32),
+            pltpu.VMEM((chunks, 2, flat), f32),
+            pltpu.SemaphoreType.DMA((4 + 2 * chunks,)),
+            pltpu.SemaphoreType.DMA((4 + 2 * chunks,)),
+        ],
+        compiler_params=pltpu.CompilerParams(collective_id=0, has_side_effects=True),
         name="edges",
-    )(costate, summary_weights())
+    )(costate, summary_weights(), costate)
 
 
 def pulled_back(density, momentum, energy, a, b):
@@ -159,7 +261,7 @@
 
 
 def main_kernel(
-    chunks, rows, density_ref, momentum_ref, energy_ref, cost_ref, ahead_ref,
+    chunks, rows, density_ref, momentum_ref, energy_ref, cost_ref, next_ref, ahead_ref,
     left_ref, right_ref, zleft_ref, zright_ref, weight_ref, rim_ref,
     out_ref, back_ref, span_ref, carry_ref,
 ):
@@ -173,10 +275,6 @@
         carry_ref[...] = left_ref[...]
 
     last = step == chunks - 1
-    scale = f32(0.0)
-    for k in range(chunks):
-        scale = jnp.where(step == k, f32(root ** (rows * (chunks - 1 - k))), scale)
-    keep = jnp.where(last, f32(1.0), f32(0.0))
 
     def times(high, low, kind):
         dot = functools.partial(jnp.dot, preferred_element_type=f32)
@@ -209,8 +307,8 @@
         tiles[-1] += part[:, 128:]
         for t, tile in enumerate(tiles):
             span_ref[field, :, :, t * 128 : (t + 1) * 128] = tile.reshape(rows, planes, 128)
-        back = ahead_ref[0, 0, field] + scale * right_ref[0, field]
-        ahead = ahead_ref[0, 1, field] + keep * right_ref[1, field]
+        back = ahead_ref[0, field]
+        ahead = jnp.where(last, right_ref[field], next_ref[field, 0])
         for i in reversed(range(rows)):
             back_ref[field, i] = tail * back + near * ahead
             ahead = cost_ref[field, i]
@@ -263,7 +361,11 @@
         grid=(chunks,),
         in_specs=[
             state, stacked(3), state, stacked(fields),
-            pl.BlockSpec((1,) + layer, lambda s: (s, 0, 0, 0, 0)),
+            pl.BlockSpec(
+                (fields, 1, planes, lanes),
+                lambda s: (0, jnp.minimum(rows * (s + 1), length - 1), 0, 0),
+            ),
+            pl.BlockSpec((1,) + layer[1:], lambda s: (s, 0, 0, 0)),
             whole(left), whole(right), strip, strip, whole(weights), whole(rim),
         ],
         out_specs=stacked(fields),
@@ -274,21 +376,12 @@
             pltpu.VMEM(layer, f32),
         ],
         name="pull",
-    )(density, momentum, energy, costate, ahead, left, right, zleft, zright, weights, rim)
+    )(density, momentum, energy, costate, costate, ahead, left, right, zleft, zright, weights, rim)
 
 
 def per_device(density, momentum, energy, costate):
     rows = 32
-    ahead, up, down, zup, zdown = edges(costate, rows)
-
-    def shifted(values, axis, by):
-        peers = lax.axis_size(axis)
-        return lax.ppermute(values, axis, [(i, (i + by) % peers) for i in range(peers)])
-
-    left = shifted(up, "gx", 1)
-    right = shifted(down, "gx", -1)
-    zleft = shifted(zup, "gz", 1)
-    zright = shifted(zdown, "gz", -1)
+    ahead, left, right, zleft, zright = edges(costate, rows)
     return main(density, momentum, energy, costate, ahead, left, right, zleft, zright, rows)
 
 

time: 58.9 us -> 56.7 us (0.963)
  Pallas kernels: 45.8 us -> 56.5 us
  starting transfers between devices: 7.62 us -> 0 us
  waiting for transfers between devices: 4.5 us -> 0 us
  local copies, waits for them, and re-layouts: 0.73 us -> 0 us
    pallas_call x1, Pallas kernels: 11.5 us -> 22 us  [edges(): pl.pallas_call(functools.partial(edges_kernel, chunks, rows), grid=(chunk...]
    ppermute x4 -> x0, starting transfers between devices: 7.62 us -> none  [shifted(): lax.ppermute(values, axis, [(i, (i + by) % peers) for i in range(peers)])]
    ppermute x4 -> x0, waiting for transfers between devices: 4.5 us -> none  [shifted(): lax.ppermute(values, axis, [(i, (i + by) % peers) for i in range(peers)])]
    unnamed x8 -> x0, local copies, waits for them, and re-layouts: 0.73 us -> none
  transfers between devices with their start and end apart: 4 -> 0, of which waited for: 2 -> 0; matrix products, arithmetic and copies ran while one was open for 0% -> 0% of each run, Pallas kernels for 0% -> 0%
where the time goes in v1:
time: 56.7 us; the launch traced here: 56.5 us
  Pallas kernels  56.5 us (100%)
    pallas_call x1, Pallas kernels, main(): pl.pallas_call(functools.partial(main_kernel, chunks, rows), grid=(chunks...  34.4 us
    pallas_call x1, Pallas kernels, edges(): pl.pallas_call(functools.partial(edges_kernel, chunks, rows), grid=(chunk...  22 us

profile of v1, /device:TPU:0, one launch (start us, length us, event | category | flops | bytes accessed | tf_op | source)
XLA Modules:
  0.0 56.5 jit_solution(5923998041790190426)
XLA Ops:
  0.0 22.0 %edges.1 = (f32[8,5,8,512]{3,2,1,0:T(8,128)}, f32[2,5,8,512]{3,2,1,0:T(8,128)}, f32[5,8,512]{2,1,0:T(8,128)}, f32[8,2,1280]{2,1,0:T(2,128)}, f32[8,2,1280]{2,1,0:T(2,128)}) custom-call(f32[5,256,8,512]{3,2,1,0:T(8,128)} %next_ref.1, bf16[2,16,128]{2,1,0:T(8,128)(2,1)} %constant.15.weight_ref, f32[5,256,8,512]{3,2,1,0:T(8,128)} %next_ref.1), custom_call_target="tpu_custom_call" | custom-call | tf_op jit(solution)/shard_map/edges/pallas_call | solution.py:206
  22.0 34.4 %pull.1 = f32[5,256,8,512]{3,2,1,0:T(8,128)} custom-call(f32[256,8,512]{2,1,0:T(8,128)} %density_ref.1, f32[3,256,8,512]{3,2,1,0:T(8,128)} %momentum_ref.1, f32[256,8,512]{2,1,0:T(8,128)} %energy_ref.1, f32[5,256,8,512]{3,2,1,0:T(8,128)} %next_ref.1, f32[5,256,8,512]{3,2,1,0:T(8,128)} %next_ref.1, f32[8,5,8,512]{3,2,1,0:T(8,128)} %get-tuple-element.10.ahead_ref, ...), custom_call_target="tpu_custom_call" | custom-call | tf_op jit(solution)/shard_map/pull/pallas_call | solution.py:359

commit v2 on v1

--- a/solution.py
+++ b/solution.py
@@ -77,13 +77,12 @@
 
 
 def edges_kernel(
-    chunks, rows, cost_ref, weight_ref, raw_ref,
+    chunks, rows, cost_ref, first_ref, final_ref, weight_ref, raw_ref,
     ahead_ref, left_ref, right_ref, zleft_ref, zright_ref,
     up_ref, down_ref, local_ref, far_ref, zup_ref, zdown_ref, send, recv,
 ):
     step = pl.program_id(0)
     fields = cost_ref.shape[0]
-    lanes = cost_ref.shape[3]
     length = raw_ref.shape[1]
     near_rows = heard(chunks, rows)
     ready = min(2 * len(near_rows), chunks)
@@ -111,10 +110,9 @@
     ]
 
     def span_copies(at):
-        chunk = visit(at, chunks)
         return [
-            remote(zup_ref.at[chunk], zleft_ref.at[chunk], 4 + at, zafter),
-            remote(zdown_ref.at[chunk], zright_ref.at[chunk], 4 + chunks + at, zbefore),
+            remote(zup_ref.at[at], zleft_ref.at[at], 4 + at, zafter),
+            remote(zdown_ref.at[at], zright_ref.at[at], 4 + chunks + at, zbefore),
         ]
 
     @pl.when(step == 0)
@@ -133,9 +131,9 @@
         for copy in rim_copies:
             copy.start()
 
-    @pl.when(step >= 1)
-    def _():
-        for copy in span_copies(step - 1):
+    @pl.when(step > chunks)
+    def _():
+        for copy in span_copies(step - 1 - chunks):
             copy.start()
 
     @pl.when(step == ready)
@@ -157,10 +155,6 @@
             for f in range(fields):
                 up_ref[f] = up_ref[f] + scale * fronts[f]
 
-        contract = functools.partial(
-            lax.dot_general, dimension_numbers=(((1,), (1,)), ((), ())),
-            preferred_element_type=jnp.float32,
-        )
         backs = [jnp.zeros_like(down_ref[f]) for f in range(fields)]
         for i in reversed(range(rows)):
             backs = [root * (cost_ref[f, i] + backs[f]) for f in range(fields)]
@@ -172,16 +166,23 @@
             def _():
                 down_ref[field] = down_ref[field] + scale * backs[field]
 
-            at = pl.ds(field * rows * 8, rows * 8)
-            for side, from_lane, ref in ((0, 0, zdown_ref), (1, lanes - 128, zup_ref)):
-                part = cost_ref[field, :, :, from_lane : from_lane + 128]
-                high, low = split(part.reshape(rows * 8, 128))
+    @pl.when((step >= chunks) & (step < 2 * chunks))
+    def _():
+        chunk = step - chunks
+        contract = functools.partial(
+            lax.dot_general, dimension_numbers=(((1,), (1,)), ((), ())),
+            preferred_element_type=jnp.float32,
+        )
+        for field in range(fields):
+            at = slice(field * rows * 8, (field + 1) * rows * 8)
+            for side, edge, ref in ((0, first_ref, zdown_ref), (1, final_ref, zup_ref)):
+                high, low = split(edge[field].reshape(rows * 8, 128))
                 both = contract(weight_ref[side], high)
                 ref[chunk, :, at] = (
                     both[0:2] + both[8:10] + contract(weight_ref[side], low)[0:2]
                 )
 
-    @pl.when(step == chunks)
+    @pl.when(step == 2 * chunks)
     def _():
         for copy in rim_copies + state_copies:
             copy.wait()
@@ -203,14 +204,19 @@
     layer = (fields, planes, lanes)
     f32 = jnp.float32
     anywhere = pl.BlockSpec(memory_space=pl.ANY)
+    later = lambda s: jnp.clip(s - chunks, 0, chunks - 1)
+    edge = lambda tile: pl.BlockSpec(
+        (fields, rows, planes, 128), lambda s: (0, later(s), 0, tile)
+    )
     return pl.pallas_call(
         functools.partial(edges_kernel, chunks, rows),
-        grid=(chunks + 1,),
+        grid=(2 * chunks + 1,),
         in_specs=[
             pl.BlockSpec(
                 (fields, rows, planes, lanes),
                 lambda s: (0, visit(jnp.minimum(s, chunks - 1), chunks), 0, 0),
             ),
+            edge(0), edge(lanes // 128 - 1),
             pl.BlockSpec((2, 16, 128), lambda s: (0, 0, 0)),
             anywhere,
         ],
@@ -237,7 +243,7 @@
         ],
         compiler_params=pltpu.CompilerParams(collective_id=0, has_side_effects=True),
         name="edges",
-    )(costate, summary_weights(), costate)
+    )(costate, costate, costate, summary_weights(), costate)
 
 
 def pulled_back(density, momentum, energy, a, b):

time: 56.7 us -> 61 us (1.076)
  Pallas kernels: 56.5 us -> 60.7 us
    pallas_call x1, Pallas kernels: 22 us -> 26.3 us  [edges(): pl.pallas_call(functools.partial(edges_kernel, chunks, rows), grid=(2 * c...]
where the time goes in v2:
time: 61 us; the launch traced here: 60.7 us
  Pallas kernels  60.7 us (100%)
    pallas_call x1, Pallas kernels, main(): pl.pallas_call(functools.partial(main_kernel, chunks, rows), grid=(chunks...  34.5 us
    pallas_call x1, Pallas kernels, edges(): pl.pallas_call(functools.partial(edges_kernel, chunks, rows), grid=(2 * c...  26.3 us

profile of v2, /device:TPU:0, one launch (start us, length us, event | category | flops | bytes accessed | tf_op | source)
XLA Modules:
  0.0 60.7 jit_solution(12872348440348182489)
XLA Ops:
  0.0 26.3 %edges.1 = (f32[8,5,8,512]{3,2,1,0:T(8,128)}, f32[2,5,8,512]{3,2,1,0:T(8,128)}, f32[5,8,512]{2,1,0:T(8,128)}, f32[8,2,1280]{2,1,0:T(2,128)}, f32[8,2,1280]{2,1,0:T(2,128)}) custom-call(f32[5,256,8,512]{3,2,1,0:T(8,128)} %next_ref.1, f32[5,256,8,512]{3,2,1,0:T(8,128)} %next_ref.1, f32[5,256,8,512]{3,2,1,0:T(8,128)} %next_ref.1, ...), custom_call_target="tpu_custom_call" | custom-call | tf_op jit(solution)/shard_map/edges/pallas_call | solution.py:211
  26.3 34.5 %pull.1 = f32[5,256,8,512]{3,2,1,0:T(8,128)} custom-call(f32[256,8,512]{2,1,0:T(8,128)} %density_ref.1, f32[3,256,8,512]{3,2,1,0:T(8,128)} %momentum_ref.1, f32[256,8,512]{2,1,0:T(8,128)} %energy_ref.1, f32[5,256,8,512]{3,2,1,0:T(8,128)} %next_ref.1, f32[5,256,8,512]{3,2,1,0:T(8,128)} %next_ref.1, f32[8,5,8,512]{3,2,1,0:T(8,128)} %get-tuple-element.10.ahead_ref, ...), custom_call_target="tpu_custom_call" | custom-call | tf_op jit(solution)/shard_map/pull/pallas_call | solution.py:365
